TPU v7x, 512 devices: a whole 4x4x16 slice. The times are simulated.
512 devices in a mesh: ctx: 64 (over y, z), head: 8 (over x, core).
Axes of the slice: x: 4, y: 4, z: 16, core: 2. Of those that a mesh axis runs over, the one named last changes fastest.
Arguments:
- lin_query: bfloat16 [8192, 64, 128], P('ctx', 'head'), may hold values from -6 to 6
- lin_key: bfloat16 [8192, 64, 128], P('ctx', 'head'), may hold values from -6 to 6
- lin_value: bfloat16 [8192, 64, 128], P('ctx', 'head'), may hold values from -18 to 18
- log_decay: float32 [64, 8192], P('head', 'ctx'), may hold values from -1 to 0
- norm_gain: float32 [64, 128], P('head'), may hold values from 0.5 to 1.5
- attn_query: bfloat16 [8192, 64, 128], P('ctx', 'head'), may hold values from -30 to 30
- attn_key: bfloat16 [8192, 8, 128], P('ctx', 'head'), may hold values from -16 to 16
- attn_value: bfloat16 [8192, 8, 128], P('ctx', 'head'), may hold values from -6 to 6
Outputs:
- lin_out: bfloat16 [8192, 64, 128], P('ctx', 'head')
- attn_out: bfloat16 [8192, 64, 128], P('ctx', 'head')
All inputs are finite; a program needn't handle non-finite values.
Results may differ from a plain program's by a relative error of at most 0.0055.
Values may be sent and summed in bfloat16 or wider, within the bound.
No kernel may reach another device: no remote copies, remote signals or barrier semaphores. Data moves between devices by JAX's collectives and lax.ppermute only.
A program may use at most 192 MiB of HBM per device.

v0:
```python
import jax
import jax.numpy as jnp
from jax import lax
from jax.sharding import PartitionSpec as P

QUERY_HEADS = 64
HD = 128


def carried_in(x, axis, combine, identity):
    size, mine = (lax.axis_size(axis), lax.axis_index(axis))
    everything = jax.tree.map(lambda part: lax.all_gather(part, axis), x)
    start = jax.tree.map(
        lambda part, zero: jnp.broadcast_to(jnp.asarray(zero, part.dtype), part.shape), x, identity
    )

    def hop(k, before):
        reached = k < mine
        new = combine(before, jax.tree.map(lambda part: part[k], everything))
        return jax.tree.map(lambda a, b: jnp.where(reached, a, b), new, before)

    return lax.fori_loop(0, size, hop, start)


def act_round(values):
    return jax.nn.silu(values.astype(jnp.float32)).astype(jnp.bfloat16)


def chain_state(earlier, later):
    decay_early, state_early = earlier
    decay_late, state_late = later
    return (decay_early * decay_late, decay_late[:, None, None] * state_early + state_late)


def lightning(lin_query, lin_key, lin_value, log_decay, norm_gain):
    act_query = act_round(lin_query)
    act_key = act_round(lin_key)
    act_value = act_round(lin_value)
    token_position = jnp.arange(lin_query.shape[0])
    cumulative = jnp.cumsum(log_decay, axis=1)
    causal = token_position[:, None] >= token_position[None, :]
    spread = cumulative[:, :, None] - cumulative[:, None, :]
    decay_matrix = jnp.exp(jnp.where(causal[None], spread, -1e30))
    scores = jnp.einsum("thd,shd->hts", act_query, act_key, preferred_element_type=jnp.float32)
    weights = (scores * decay_matrix).astype(jnp.bfloat16)
    inner_part = jnp.einsum("hts,shd->thd", weights, act_value, preferred_element_type=jnp.float32)
    last_sum = cumulative[:, -1]
    key_factor = jnp.exp(last_sum[None, :] - cumulative.T)
    scaled_keys = (act_key.astype(jnp.float32) * key_factor[:, :, None]).astype(jnp.bfloat16)
    local_state = jnp.einsum(
        "shd,she->hde", scaled_keys, act_value, preferred_element_type=jnp.float32
    )
    identity = (jnp.ones_like(last_sum), jnp.zeros_like(local_state))
    prior_decay, prior_state = carried_in(
        (jnp.exp(last_sum), local_state), "ctx", chain_state, identity
    )
    outer_part = jnp.einsum(
        "thd,hde->the", act_query.astype(jnp.float32), prior_state, precision=lax.Precision.HIGHEST
    )
    mixed_out = inner_part + outer_part * jnp.exp(cumulative.T)[:, :, None]
    row_squares = jnp.sum(mixed_out * mixed_out, axis=(1, 2))
    total_squares = lax.psum(row_squares, "head")
    inverse = lax.rsqrt(total_squares / (QUERY_HEADS * HD) + 1e-06)
    return (mixed_out * inverse[:, None, None] * norm_gain[None]).astype(jnp.bfloat16)


def to_groups(query_rows, kv_local):
    rows = query_rows.shape[0]
    group = query_rows.shape[1] // kv_local
    shaped = query_rows.reshape(rows, kv_local, group, query_rows.shape[2]).transpose(1, 0, 2, 3)
    return shaped.reshape(kv_local, rows * group, query_rows.shape[2])


def from_groups(grouped, rows):
    kv_local = grouped.shape[0]
    group = grouped.shape[1] // rows
    shaped = grouped.reshape(kv_local, rows, group, grouped.shape[2]).transpose(1, 0, 2, 3)
    return shaped.reshape(rows, kv_local * group, grouped.shape[2])


def attend(state_now, group_query, positions, key_piece, value_piece):
    running_max, totals, accumulated = state_now
    scores = jnp.einsum(
        "gqd,pgd->gqp", group_query, key_piece, preferred_element_type=jnp.float32
    ) * HD ** (-0.5)
    key_pos = jnp.arange(key_piece.shape[0])
    visible = positions[:, None] >= key_pos[None, :]
    masked = jnp.where(visible[None], scores, -1e30)
    newest = jnp.maximum(running_max, jnp.max(masked, axis=2))
    prob_rows = jnp.where(visible[None], jnp.exp(scores - newest[:, :, None]), 0.0)
    totals = jnp.sum(prob_rows, axis=2)
    accumulated = jnp.einsum(
        "gqp,pgd->gqd",
        prob_rows.astype(jnp.bfloat16),
        value_piece,
        preferred_element_type=jnp.float32,
    )
    return (newest, totals, accumulated)


def softmax_part(attn_query, attn_key, attn_value):
    length = attn_query.shape[0]
    kv_local = attn_key.shape[1]
    group = attn_query.shape[1] // kv_local
    ctx_index = lax.axis_index("ctx")
    own_pos = ctx_index * length + jnp.arange(length)
    query_sets = [(to_groups(attn_query, kv_local), jnp.repeat(own_pos, group), length)]

    def empty_state(group_query):
        shape_rows = group_query.shape[:2]
        return (
            jnp.full(shape_rows, -1e30, jnp.float32),
            jnp.zeros(shape_rows, jnp.float32),
            jnp.zeros(group_query.shape, jnp.float32),
        )

    initial = tuple((empty_state(query_set[0]) for query_set in query_sets))
    key_piece = lax.all_gather(attn_key, "ctx", axis=0, tiled=True)
    value_piece = lax.all_gather(attn_value, "ctx", axis=0, tiled=True)
    results = []
    for query_set, state_now in zip(query_sets, initial):
        group_query, positions, set_rows = query_set
        state_now = attend(state_now, group_query, positions, key_piece, value_piece)
        results.append(state_now)
    finals = tuple(results)
    running_max, totals, accumulated = finals[0]
    grouped = (accumulated / totals[:, :, None]).astype(jnp.bfloat16)
    result = from_groups(grouped, length)
    return result


def local(lin_query, lin_key, lin_value, log_decay, norm_gain, attn_query, attn_key, attn_value):
    lin_out = lightning(lin_query, lin_key, lin_value, log_decay, norm_gain)
    attn_out = softmax_part(attn_query, attn_key, attn_value)
    return (lin_out, attn_out)


def solution(mesh):
    return jax.shard_map(
        local,
        mesh=mesh,
        in_specs=(
            P("ctx", "head", None),
            P("ctx", "head", None),
            P("ctx", "head", None),
            P("head", "ctx"),
            P("head", None),
            P("ctx", "head", None),
            P("ctx", "head", None),
            P("ctx", "head", None),
        ),
        out_specs=(P("ctx", "head", None), P("ctx", "head", None)),
        check_vma=False,
    )
```

profile of v0, /device:TPU:1, one launch (start us, length us, event | category | flops | bytes accessed | tf_op | source)
XLA Modules:
  0.0 689.5 jit_solution(787471788955299901)
XLA Ops:
  10.0 1.4 multiply_convert_fusion.1
  12.5 1.3 dynamic-slice
  14.7 123.1 %all-reduce = f32[512]{0:T(512)S(1)} all-reduce(f32[512]{0:T(512)S(1)} %dynamic-update-slice), channel_id=2, replica_groups=mesh['ctx'=64,'head'=8] {'ctx'}, use_global_device_ids=true, to_apply=%add | all-reduce | flops 512 | bytes 4096
  139.3 9.0 %all-gather.6.cloned.1.call-done = bf16[8192,1,128]{2,0,1:T(8,128)(2,1)} async-done(((bf16[128,1,128]{2,0,1:T(8,128)(2,1)}), bf16[8192,1,128]{2,0,1:T(8,128)(2,1)}) %all-gather.6.cloned.1.call-update) | async-done | bytes 2097168 | tf_op jit(solution)/shard_map/all_gather | solution.py:118
  148.3 15.5 %select_reduce_fusion = (f32[1024]{0:T(1024)S(1)}, f32[1024,8192]{1,0:T(8,128)}) fusion(s32[1024]{0:T(1024)S(1)} %ge.35, bf16[8192,1,128]{2,0,1:T(8,128)(2,1)} %all-gather.6.cloned.1.call-done, bf16[128,8,128]{2,1,0:T(8,128)(2,1)S(1)} %copy-done), kind=kOutput, calls=%fused_computation.4 | convolution fusion | flops 2181037056 | bytes 35921920 | tf_op jit(solution)/shard_map/gqd,pgd->gqp/dot_general | solution.py:83
  163.8 15.6 %fusion.1 = f32[1024]{0:T(1024)S(1)} fusion(f32[1024,8192]{1,0:T(8,128)} %get-tuple-element.140, f32[1024]{0:T(1024)S(1)} %broadcast_maximum_fusion, s32[1024]{0:T(1024)S(1)} %ge.35), kind=kLoop, calls=%fused_computation.6 | loop fusion | flops 41942016 | bytes 33566720 | tf_op jit(solution)/shard_map/reduce_sum | solution.py:91
  179.4 108.9 %all-gather.8.cloned.1.call-done = bf16[8192,1,128]{2,0,1:T(8,128)(2,1)} async-done(((bf16[128,1,128]{2,0,1:T(8,128)(2,1)}), bf16[8192,1,128]{2,0,1:T(8,128)(2,1)}) %all-gather.8.cloned.1.call-update) | async-done | bytes 2097168 | tf_op jit(solution)/shard_map/all_gather | solution.py:119
  288.3 15.6 %fusion.21 = bf16[128,8,128]{2,1,0:T(8,128)(2,1)} fusion(bf16[8192,1,128]{2,0,1:T(8,128)(2,1)} %all-gather.8.cloned.1.call-done, f32[1024,8192]{1,0:T(8,128)} %get-tuple-element.140, f32[1024]{0:T(1024)S(1)} %broadcast_maximum_fusion, s32[1024]{0:T(1024)S(1)} %ge.35, f32[1024]{0:T(1024)S(1)} %fusion.1), kind=kOutput, calls=%fused_computation.20 | convolution fusion | flops 2189688832 | bytes 35926016 | tf_op jit(solution)/shard_map/gqp,pgd->gqd/dot_general | solution.py:92
  303.8 286.3 %all-gather.10.cloned.1.call-done = f32[512,128,128]{2,1,0:T(8,128)} async-done(((f32[8,128,128]{2,1,0:T(8,128)}), f32[512,128,128]{2,1,0:T(8,128)}) %all-gather.10.cloned.1.call-update) | async-done | bytes 33554448 | tf_op jit(solution)/shard_map/all_gather | solution.py:12
  590.1 77.7 %while.14 = (s32[]{:T(128)}, f32[8,128,128]{2,1,0:T(8,128)S(1)}, s32[]{:T(128)}, f32[64,8]{1,0:T(8,128)S(1)}, f32[64,8,128,128]{3,2,1,0:T(8,128)}, /*index=5*/s32[]{:T(128)}, s32[]{:T(128)}) while((s32[]{:T(128)}, f32[8,128,128]{2,1,0:T(8,128)S(1)}, s32[]{:T(128)}, f32[64,8]{1,0:T(8,128)S(1)}, f32[64,8,128,128]{3,2,1,0:T(8,128)}, ...), condition=%wide.region_2.3_spmd.clone, body=%wide.region_1.2_spmd.clone.sunk | while | flops 524292 | bytes 1573065 | solution.py:22
  591.4 1.2 fusion.65
  592.6 1.2 fusion.65
  593.8 1.2 fusion.65
  595.0 1.2 fusion.65
  596.2 1.2 fusion.65
  597.4 1.2 fusion.65
  598.6 1.2 fusion.65
  599.9 1.2 fusion.65
  602.3 1.2 fusion.65
  604.7 1.2 fusion.65
  605.9 1.2 fusion.65
  607.1 1.2 fusion.65
  608.4 1.2 fusion.65
  609.6 1.2 fusion.65
  610.8 1.2 fusion.65
  612.0 1.2 fusion.65
  613.2 1.2 fusion.65
  614.4 1.2 fusion.65
  615.6 1.2 fusion.65
  616.8 1.2 fusion.65
  618.1 1.2 fusion.65
  619.3 1.2 fusion.65
  620.5 1.2 fusion.65
  621.7 1.2 fusion.65
  622.9 1.2 fusion.65
  625.3 1.2 fusion.65
  627.8 1.2 fusion.65
  629.0 1.2 fusion.65
  630.2 1.2 fusion.65
  631.4 1.2 fusion.65
  632.6 1.2 fusion.65
  633.8 1.2 fusion.65
  635.1 1.2 fusion.65
  636.3 1.2 fusion.65
  637.5 1.2 fusion.65
  638.7 1.2 fusion.65
  639.9 1.2 fusion.65
  669.0 12.9 %psum.7 = f32[128]{0:T(128)S(1)} all-reduce(f32[128]{0:T(128)S(1)} %get-tuple-element.137), channel_id=1, replica_groups=mesh['ctx'=64,'head'=8] {'head'}, use_global_device_ids=true, to_apply=%region_4.5 | all-reduce | flops 128 | bytes 1024 | tf_op jit(solution)/shard_map/psum | solution.py:62
  (123 shorter events, 40.1 us)
Async XLA Ops:
  7.2 141.1 %copy-start = (bf16[128,8,128]{2,1,0:T(8,128)(2,1)S(1)}, bf16[128,8,128]{2,1,0:T(8,128)(2,1)}, u32[]{:S(2)}) copy-start(bf16[128,8,128]{2,1,0:T(8,128)(2,1)} %param.15) | copy-start | bytes 786436
  7.2 141.1 %all-gather.6.cloned.1.call-start = ((), (), s32[]{:S(2)}) async-start(), calls=%async_computation | async-start | bytes 2129920 | tf_op jit(solution)/shard_map/all_gather | solution.py:118
  7.9 280.4 %all-gather.8.cloned.1.call-start = ((), (), s32[]{:S(2)}) async-start(), calls=%async_computation.1 | async-start | bytes 2129920 | tf_op jit(solution)/shard_map/all_gather | solution.py:119
  8.7 581.5 %all-gather.10.cloned.1.call-start = ((), (), s32[]{:S(2)}) async-start(), calls=%async_computation.2 | async-start | bytes 34078720 | tf_op jit(solution)/shard_map/all_gather | solution.py:12
  163.8 519.2 %copy-start.1 = (bf16[128,8,128]{2,1,0:T(8,128)(2,1)S(1)}, bf16[128,8,128]{2,1,0:T(8,128)(2,1)}, u32[]{:S(2)}) copy-start(bf16[128,8,128]{2,1,0:T(8,128)(2,1)} %param.15) | copy-start | bytes 786436
  179.4 502.4 %copy-start.2 = (f32[8,128]{1,0:T(8,128)S(1)}, f32[8,128]{1,0:T(8,128)}, u32[]{:S(2)}) copy-start(f32[8,128]{1,0:T(8,128)} %param.14) | copy-start | bytes 12292
Sparse Core Ops, SparseCore 0:
  11.0 137.2 all-gather.5
  151.2 136.9 all-gather.7
  291.2 298.8 all-gather.9
where the time goes:
time: 693 us; the launch traced here: 689 us
  waiting for transfers between devices  406 us (59%)
  blocking collectives  136 us (20%)
  other arithmetic  94.4 us (14%)
  matrix products  33.2 us (5%)
  between operations  14.5 us (2%)
    all_gather x1, waiting for transfers between devices, carried_in(): everything = jax.tree.map(lambda part: lax.all_gather(part, axis), x)  286 us
    unnamed x1, blocking collectives  123 us
    all_gather x1, waiting for transfers between devices, softmax_part(): value_piece = lax.all_gather(attn_value, 'ctx', axis=0, tiled=True)  109 us
    select_n x64, other arithmetic, hop(): return jax.tree.map(lambda a, b: jnp.where(reached, a, b), new, before)  75.1 us
    reduce_sum x1, other arithmetic, attend(): totals = jnp.sum(prob_rows, axis=2)  15.6 us
    dot_general x1, matrix products, attend(): jnp.einsum('gqp,pgd->gqd', prob_rows.astype(jnp.bfloat16), value_piece, p...  15.6 us
    dot_general x1, matrix products, attend(): jnp.einsum('gqd,pgd->gqp', group_query, key_piece, preferred_element_type...  15.5 us
  transfers between devices with their start and end apart: 3, of which 3 were waited for; matrix products, arithmetic and copies ran while one was open for 8% of the time, Pallas kernels for 0%

commit v1 on v0

--- a/solution.py
+++ b/solution.py
@@ -116,7 +116,12 @@
 
     initial = tuple((empty_state(query_set[0]) for query_set in query_sets))
     key_piece = lax.all_gather(attn_key, "ctx", axis=0, tiled=True)
-    value_piece = lax.all_gather(attn_value, "ctx", axis=0, tiled=True)
+    n = lax.axis_size("ctx")
+    steps_seen = []
+    for nth in tuple(range(attn_value.ndim)):
+        steps_seen.append(n if nth == 0 else 1)
+    plain = jnp.tile(attn_value, steps_seen)
+    value_piece = lax.all_to_all(plain, "ctx", tiled=True, split_axis=0, concat_axis=0)
     results = []
     for query_set, state_now in zip(query_sets, initial):
         group_query, positions, set_rows = query_set

time: 693 us -> 577 us (0.83)
  waiting for transfers between devices: 406 us -> 178 us
  blocking collectives: 136 us -> 211 us
  starting transfers between devices: 0.11 us -> 19.4 us
  local copies, waits for them, and re-layouts: 3.57 us -> 16.1 us
    all_gather x1 -> x0, waiting for transfers between devices: 109 us -> none  [softmax_part(): value_piece = lax.all_gather(attn_value, 'ctx', axis=0, tiled=True)]
    all_gather x1, waiting for transfers between devices: 286 us -> 177 us  [carried_in(): everything = jax.tree.map(lambda part: lax.all_gather(part, axis), x)]
    unnamed x1, blocking collectives: 123 us -> 198 us
    all_to_all x0 -> x1, starting transfers between devices: none -> 19.3 us  [softmax_part(): lax.all_to_all(plain, 'ctx', tiled=True, split_axis=0, concat_axis=0)]
    unnamed x10 -> x14, local copies, waits for them, and re-layouts: 2.42 us -> 13.2 us
    all_gather x1, waiting for transfers between devices: 9.04 us -> 0.02 us  [softmax_part(): key_piece = lax.all_gather(attn_key, 'ctx', axis=0, tiled=True)]
  transfers between devices with their start and end apart: 3 -> 3, of which waited for: 3 -> 1; matrix products, arithmetic and copies ran while one was open for 8% -> 12% of each run, Pallas kernels for 0% -> 0%
where the time goes in v1:
time: 577 us; the launch traced here: 574 us
  blocking collectives  211 us (37%)
  waiting for transfers between devices  178 us (31%)
  other arithmetic  98 us (17%)
  matrix products  34.4 us (6%)
  starting transfers between devices  19.4 us (3%)
  local copies, waits for them, and re-layouts  16.1 us (3%)
  between operations  14.9 us (3%)
    unnamed x1, blocking collectives  198 us
    all_gather x1, waiting for transfers between devices, carried_in(): everything = jax.tree.map(lambda part: lax.all_gather(part, axis), x)  177 us
    select_n x64, other arithmetic, hop(): return jax.tree.map(lambda a, b: jnp.where(reached, a, b), new, before)  75.2 us
    all_to_all x1, starting transfers between devices, softmax_part(): lax.all_to_all(plain, 'ctx', tiled=True, split_axis=0, concat_axis=0)  19.3 us
    dot_general x1, matrix products, attend(): jnp.einsum('gqp,pgd->gqd', prob_rows.astype(jnp.bfloat16), value_piece, p...  16.7 us
    reduce_sum x1, other arithmetic, attend(): totals = jnp.sum(prob_rows, axis=2)  15.6 us
    dot_general x1, matrix products, attend(): jnp.einsum('gqd,pgd->gqp', group_query, key_piece, preferred_element_type...  15.5 us
    unnamed x14, local copies, waits for them, and re-layouts  13.2 us
  transfers between devices with their start and end apart: 3, of which 1 were waited for; matrix products, arithmetic and copies ran while one was open for 12% of the time, Pallas kernels for 0%

profile of v1, /device:TPU:1, one launch (start us, length us, event | category | flops | bytes accessed | tf_op | source)
XLA Modules:
  0.0 573.5 jit_solution(8702593161325133710)
XLA Ops:
  9.3 1.9 multiply_convert_fusion.1
  12.3 1.3 tile.12
  14.1 2.9 reduce.8
  17.0 4.0 reshape.92
  21.0 19.3 %all-to-all-start = ((bf16[64,2,8192]{2,1,0:T(2,128)(2,1)}), bf16[64,2,8192]{2,1,0:T(2,128)(2,1)S(1)}, u32[]{:S(2)}, u32[]{:S(2)}) async-start(bf16[64,2,8192]{2,1,0:T(2,128)(2,1)} %reshape.92), calls=%async_computation | async-start | bytes 4194304 | tf_op jit(solution)/shard_map/all_to_all | solution.py:124
  40.3 1.3 dynamic-slice
  42.5 197.7 %all-reduce = f32[512]{0:T(512)S(1)} all-reduce(f32[512]{0:T(512)S(1)} %dynamic-update-slice), channel_id=2, replica_groups=mesh['ctx'=64,'head'=8] {'ctx'}, use_global_device_ids=true, to_apply=%add | all-reduce | flops 512 | bytes 4096
  241.6 15.5 %select_reduce_fusion = (f32[1024]{0:T(1024)S(1)}, f32[1024,8192]{1,0:T(8,128)}) fusion(s32[1024]{0:T(1024)S(1)} %ge.35, bf16[8192,1,128]{2,0,1:T(8,128)(2,1)} %all-gather.5.cloned.1.call-done, bf16[128,8,128]{2,1,0:T(8,128)(2,1)S(1)} %copy-done), kind=kOutput, calls=%fused_computation.4 | convolution fusion | flops 2181037056 | bytes 35921920 | tf_op jit(solution)/shard_map/gqd,pgd->gqp/dot_general | solution.py:83
  257.1 15.6 %fusion.1 = f32[1024]{0:T(1024)S(1)} fusion(f32[1024,8192]{1,0:T(8,128)} %get-tuple-element.142, f32[1024]{0:T(1024)S(1)} %broadcast_maximum_fusion, s32[1024]{0:T(1024)S(1)} %ge.35), kind=kLoop, calls=%fused_computation.6 | loop fusion | flops 41942016 | bytes 33566720 | tf_op jit(solution)/shard_map/reduce_sum | solution.py:91
  272.7 6.8 %reshape.93 = bf16[8192,1,128]{2,1,0:T(2,128)(2,1)} reshape(bf16[64,2,8192]{2,1,0:T(2,128)(2,1)S(1)} %all-to-all-done) | data formatting | bytes 4194304
  279.4 16.7 %fusion.22 = bf16[128,8,128]{2,1,0:T(8,128)(2,1)} fusion(bf16[8192,1,128]{2,1,0:T(2,128)(2,1)} %reshape.93, f32[1024,8192]{1,0:T(8,128)} %get-tuple-element.142, f32[1024]{0:T(1024)S(1)} %broadcast_maximum_fusion, s32[1024]{0:T(1024)S(1)} %ge.35, f32[1024]{0:T(1024)S(1)} %fusion.1), kind=kOutput, calls=%fused_computation.21 | convolution fusion | flops 2189688832 | bytes 35926016 | tf_op jit(solution)/shard_map/gqp,pgd->gqd/dot_general | solution.py:92
  296.2 177.5 %all-gather.7.cloned.1.call-done = f32[512,128,128]{2,1,0:T(8,128)} async-done(((f32[8,128,128]{2,1,0:T(8,128)}), f32[512,128,128]{2,1,0:T(8,128)}) %all-gather.7.cloned.1.call-update) | async-done | bytes 33554448 | tf_op jit(solution)/shard_map/all_gather | solution.py:12
  473.6 77.9 %while.14 = (s32[]{:T(128)}, f32[8,128,128]{2,1,0:T(8,128)S(1)}, s32[]{:T(128)}, f32[64,8]{1,0:T(8,128)S(1)}, f32[64,8,128,128]{3,2,1,0:T(8,128)}, /*index=5*/s32[]{:T(128)}, s32[]{:T(128)}) while((s32[]{:T(128)}, f32[8,128,128]{2,1,0:T(8,128)S(1)}, s32[]{:T(128)}, f32[64,8]{1,0:T(8,128)S(1)}, f32[64,8,128,128]{3,2,1,0:T(8,128)}, ...), condition=%wide.region_2.3_spmd.clone, body=%wide.region_1.2_spmd.clone.sunk | while | flops 524292 | bytes 1573073 | solution.py:22
  474.9 1.2 fusion.66
  476.1 1.2 fusion.66
  477.3 1.2 fusion.66
  478.5 1.2 fusion.66
  479.7 1.2 fusion.66
  480.9 1.2 fusion.66
  482.2 1.2 fusion.66
  483.4 1.2 fusion.66
  485.8 1.2 fusion.66
  487.0 1.2 fusion.66
  490.7 1.2 fusion.66
  491.9 1.2 fusion.66
  495.6 1.2 fusion.66
  499.2 1.2 fusion.66
  500.4 1.2 fusion.66
  504.1 1.2 fusion.66
  505.3 1.2 fusion.66
  509.0 1.2 fusion.66
  510.2 1.2 fusion.66
  513.8 1.2 fusion.66
  515.0 1.2 fusion.66
  518.7 1.2 fusion.66
  522.4 1.2 fusion.66
  523.6 1.2 fusion.66
  527.2 1.2 fusion.66
  528.4 1.2 fusion.66
  532.1 1.2 fusion.66
  533.3 1.2 fusion.66
  537.0 1.2 fusion.66
  538.2 1.2 fusion.66
  541.8 1.2 fusion.66
  545.5 1.2 fusion.66
  546.7 1.2 fusion.66
  550.4 1.2 fusion.66
  552.7 12.9 %psum.7 = f32[128]{0:T(128)S(1)} all-reduce(f32[128]{0:T(128)S(1)} %get-tuple-element.139), channel_id=1, replica_groups=mesh['ctx'=64,'head'=8] {'head'}, use_global_device_ids=true, to_apply=%region_4.5 | all-reduce | flops 128 | bytes 1024 | tf_op jit(solution)/shard_map/psum | solution.py:62
  (129 shorter events, 43.5 us)
Async XLA Ops:
  7.2 234.4 %copy-start = (bf16[128,8,128]{2,1,0:T(8,128)(2,1)S(1)}, bf16[128,8,128]{2,1,0:T(8,128)(2,1)}, u32[]{:S(2)}) copy-start(bf16[128,8,128]{2,1,0:T(8,128)(2,1)} %param.15) | copy-start | bytes 786436
  7.2 234.4 %all-gather.5.cloned.1.call-start = ((), (), s32[]{:S(2)}) async-start(), calls=%async_computation.1 | async-start | bytes 2129920 | tf_op jit(solution)/shard_map/all_gather | solution.py:118
  7.9 465.7 %all-gather.7.cloned.1.call-start = ((), (), s32[]{:S(2)}) async-start(), calls=%async_computation.2 | async-start | bytes 34078720 | tf_op jit(solution)/shard_map/all_gather | solution.py:12
  21.0 251.7 %all-to-all-start = ((bf16[64,2,8192]{2,1,0:T(2,128)(2,1)}), bf16[64,2,8192]{2,1,0:T(2,128)(2,1)S(1)}, u32[]{:S(2)}, u32[]{:S(2)}) async-start(bf16[64,2,8192]{2,1,0:T(2,128)(2,1)} %reshape.92), calls=%async_computation | async-start | bytes 4194304 | tf_op jit(solution)/shard_map/all_to_all | solution.py:124
  272.6 294.0 %copy-start.1 = (bf16[128,8,128]{2,1,0:T(8,128)(2,1)S(1)}, bf16[128,8,128]{2,1,0:T(8,128)(2,1)}, u32[]{:S(2)}) copy-start(bf16[128,8,128]{2,1,0:T(8,128)(2,1)} %param.15) | copy-start | bytes 786436
  279.4 272.7 %copy-start.2 = (bf16[128,8,128]{2,1,0:T(8,128)(2,1)S(1)}, bf16[128,8,128]{2,1,0:T(8,128)(2,1)}, u32[]{:S(2)}) copy-start(bf16[128,8,128]{2,1,0:T(8,128)(2,1)} %get-tuple-element.136) | copy-start | bytes 786436
  279.4 286.1 %copy-start.3 = (f32[8,128]{1,0:T(8,128)S(1)}, f32[8,128]{1,0:T(8,128)}, u32[]{:S(2)}) copy-start(f32[8,128]{1,0:T(8,128)} %param.14) | copy-start | bytes 12292
Sparse Core Ops, SparseCore 0:
  11.0 161.7 all-gather.4
  175.7 297.8 all-gather.6
